TPU v7x, 32 devices: a whole 2x2x4 slice. The times are simulated.
32 devices in a mesh: req: 4 (over y, x), head: 8 (over z, core).
Axes of the slice: x: 2, y: 2, z: 4, core: 2. Of those that a mesh axis runs over, the one named last changes fastest.
Arguments:
- hidden: bfloat16 [4, 256, 5120], P('req', 'head'), may hold values from -6 to 6
- cached_len: int32 [4], P('req'), may hold values from 2 to 4096, as said below
- attn_gain: float32 [5120], replicated, may hold values from 0.5 to 1.5
- query_key_value_weight: bfloat16 [5120, 6144], P(None, 'head'), may hold values from -0.078125 to 0.078125
- b_qkv: bfloat16 [6144], P('head'), may hold values from -1.5 to 1.5
- key_cache: bfloat16 [4, 4096, 1024], P('req', 'head'), may hold values from -4000 to 4000
- value_cache: bfloat16 [4, 4096, 1024], P('req', 'head'), may hold values from -6 to 6
- w_out: bfloat16 [4096, 5120], P('head'), may hold values from -0.09375 to 0.09375
- ffn_gain: float32 [5120], replicated, may hold values from 0.5 to 1.5
- w_gate: bfloat16 [5120, 13824], P(None, 'head'), may hold values from -0.078125 to 0.078125
- w_up: bfloat16 [5120, 13824], P(None, 'head'), may hold values from -0.078125 to 0.078125
- w_down: bfloat16 [13824, 5120], P('head'), may hold values from -0.0546875 to 0.0546875
Outputs:
- layer_out: bfloat16 [4, 256, 5120], P('req', 'head')
- new_keys: bfloat16 [4, 256, 1024], P('req', 'head')
- new_values: bfloat16 [4, 256, 1024], P('req', 'head')
Inputs may be any that keep to these rules, and one draw needn't show every extreme that they name: `cached_len`: about half of the requests have nearly full caches, within 512 of 4096, one of them exactly 4096; the others hold fewer than 512 positions; which requests are which is drawn.
All inputs are finite; a program needn't handle non-finite values.
Results may differ from a plain program's by a relative error of at most 0.015.
Values may be sent and summed in bfloat16 or wider, within the bound.
A program may use at most 256 MiB of HBM per device.

v0:
```python
import math
import jax
import jax.numpy as jnp
from jax import lax
from jax.sharding import PartitionSpec as P

QUERY_HEADS = 32
KEY_VALUE_HEADS = 8
HEAD_WIDTH = 128
rope_base = 1000000.0


def rms_norm(values, gain):
    data = values.astype(jnp.float32)
    spread = jnp.mean(data * data, axis=-1, keepdims=True)
    return (data * lax.rsqrt(spread + 1e-06) * gain).astype(jnp.bfloat16)


def rope_apply(values, positions):
    half_dim = HEAD_WIDTH // 2
    inverse = rope_base ** (-(jnp.arange(half_dim, dtype=jnp.float32) * 2.0 / HEAD_WIDTH))
    angles = positions.astype(jnp.float32)[:, None] * inverse[None, :]
    cosine = jnp.concatenate([jnp.cos(angles), jnp.cos(angles)], axis=-1)[:, None, :]
    sine = jnp.concatenate([jnp.sin(angles), jnp.sin(angles)], axis=-1)[:, None, :]
    data = values.astype(jnp.float32)
    rotated = jnp.concatenate([-data[..., half_dim:], data[..., :half_dim]], axis=-1)
    return (data * cosine + rotated * sine).astype(jnp.bfloat16)


def on_device(
    hidden,
    cached_len,
    attn_gain,
    query_key_value_weight,
    b_qkv,
    key_cache,
    value_cache,
    w_out,
    ffn_gain,
    w_gate,
    w_up,
    w_down,
):
    group_size = lax.axis_size("head")
    index_here = lax.axis_index("head")
    own_rows = hidden[0]
    fresh_count = own_rows.shape[0]
    all_rows = lax.all_gather(own_rows, "head", axis=0, tiled=True)
    token_total = all_rows.shape[0]
    head_group = QUERY_HEADS // KEY_VALUE_HEADS
    heads_here = QUERY_HEADS // group_size
    scale = 1.0 / math.sqrt(HEAD_WIDTH)
    normed = rms_norm(all_rows, attn_gain)
    qkv_part = (
        jnp.dot(normed, query_key_value_weight, preferred_element_type=jnp.float32)
        + b_qkv.astype(jnp.float32)
    ).astype(jnp.bfloat16)
    query_key_value = lax.all_gather(qkv_part, "head", axis=1, tiled=True)
    query_rows = query_key_value[:, : QUERY_HEADS * HEAD_WIDTH].reshape(
        token_total, QUERY_HEADS, HEAD_WIDTH
    )
    fresh_keys = query_key_value[
        :, QUERY_HEADS * HEAD_WIDTH : (QUERY_HEADS + KEY_VALUE_HEADS) * HEAD_WIDTH
    ].reshape(token_total, KEY_VALUE_HEADS, HEAD_WIDTH)
    fresh_values = query_key_value[:, (QUERY_HEADS + KEY_VALUE_HEADS) * HEAD_WIDTH :].reshape(
        token_total, KEY_VALUE_HEADS, HEAD_WIDTH
    )
    token_ids = jnp.arange(token_total, dtype=jnp.int32)
    positions = cached_len[0] + token_ids
    query_rows = rope_apply(query_rows, positions)
    fresh_keys = rope_apply(fresh_keys, positions)
    row_start = index_here * fresh_count
    request_keys = lax.dynamic_slice_in_dim(fresh_keys, row_start, fresh_count, 0)
    request_values = lax.dynamic_slice_in_dim(fresh_values, row_start, fresh_count, 0)
    key_lines = request_keys.reshape(1, fresh_count, KEY_VALUE_HEADS * HEAD_WIDTH)
    value_lines = request_values.reshape(1, fresh_count, KEY_VALUE_HEADS * HEAD_WIDTH)
    cache_length = key_cache.shape[1]
    joined_keys = jnp.concatenate(
        [key_cache[0].reshape(cache_length, KEY_VALUE_HEADS, HEAD_WIDTH), request_keys], axis=0
    )
    joined_values = jnp.concatenate(
        [value_cache[0].reshape(cache_length, KEY_VALUE_HEADS, HEAD_WIDTH), request_values], axis=0
    )
    cache_ok = index_here * cache_length + jnp.arange(cache_length, dtype=jnp.int32) < cached_len[0]
    own_ids = row_start + jnp.arange(fresh_count, dtype=jnp.int32)
    new_ok = own_ids[None, :] <= token_ids[:, None]
    allowed = jnp.concatenate(
        [jnp.broadcast_to(cache_ok[None, :], (token_total, cache_length)), new_ok], axis=1
    )
    grouped_queries = query_rows.reshape(token_total, KEY_VALUE_HEADS, head_group, HEAD_WIDTH)
    scores = (
        jnp.einsum(
            "tkjd,skd->kjts", grouped_queries, joined_keys, preferred_element_type=jnp.float32
        )
        * scale
    )
    scores = jnp.where(allowed[None, None], scores, -1e30)
    row_max = jnp.max(scores, axis=-1)
    expo = jnp.where(allowed[None, None], jnp.exp(scores - row_max[..., None]), 0.0)
    row_sum = jnp.sum(expo, axis=-1)
    weights = expo.astype(jnp.bfloat16)
    weighted = jnp.einsum(
        "kjts,skd->tkjd", weights, joined_values, preferred_element_type=jnp.float32
    )
    weighted = weighted.reshape(token_total, QUERY_HEADS, HEAD_WIDTH)
    row_max = jnp.transpose(row_max, (2, 0, 1)).reshape(token_total, QUERY_HEADS)
    row_sum = jnp.transpose(row_sum, (2, 0, 1)).reshape(token_total, QUERY_HEADS)
    sums_got, max_got, total_got = (
        lax.all_to_all(
            weighted[None].astype(jnp.bfloat16), "head", split_axis=2, concat_axis=0, tiled=True
        ).astype(jnp.float32),
        lax.all_to_all(
            row_max[None].astype(jnp.bfloat16), "head", split_axis=2, concat_axis=0, tiled=True
        ).astype(jnp.float32),
        lax.all_to_all(
            row_sum[None].astype(jnp.bfloat16), "head", split_axis=2, concat_axis=0, tiled=True
        ).astype(jnp.float32),
    )
    joint = jnp.max(max_got, axis=0)
    factor = jnp.exp(max_got - joint[None])
    total_here = jnp.sum(total_got * factor, axis=0)
    sums_here = jnp.sum(sums_got * factor[..., None], axis=0)
    attn = (
        (sums_here / total_here[..., None])
        .astype(jnp.bfloat16)
        .reshape(token_total, heads_here * HEAD_WIDTH)
    )
    projected = jnp.dot(attn, w_out, preferred_element_type=jnp.float32)
    projected = lax.psum(projected.astype(jnp.bfloat16), "head").astype(jnp.float32)
    middle = (all_rows.astype(jnp.float32) + projected).astype(jnp.bfloat16)
    normed_two = rms_norm(middle, ffn_gain)
    middle_own = lax.dynamic_slice_in_dim(middle, row_start, fresh_count, 0)
    gate = jnp.dot(normed_two, w_gate, preferred_element_type=jnp.float32)
    upward = jnp.dot(normed_two, w_up, preferred_element_type=jnp.float32)
    active = (jax.nn.silu(gate) * upward).astype(jnp.bfloat16)
    ffn_part = lax.psum_scatter(
        jnp.dot(active, w_down, preferred_element_type=jnp.float32).astype(jnp.bfloat16),
        "head",
        scatter_dimension=0,
        tiled=True,
    ).astype(jnp.float32)
    result = (middle_own.astype(jnp.float32) + ffn_part).astype(jnp.bfloat16)
    return (result[None], key_lines, value_lines)


def solution(mesh):
    in_specs = (
        P("req", "head", None),
        P("req"),
        P(),
        P(None, "head"),
        P("head"),
        P("req", "head", None),
        P("req", "head", None),
        P("head", None),
        P(),
        P(None, "head"),
        P(None, "head"),
        P("head", None),
    )
    out_specs = (P("req", "head", None), P("req", "head", None), P("req", "head", None))
    return jax.shard_map(
        on_device, mesh=mesh, in_specs=in_specs, out_specs=out_specs, check_vma=False
    )
```

profile of v0, /device:TPU:0, one launch (start us, length us, event | category | flops | bytes accessed | tf_op | source)
XLA Modules:
  0.0 385.5 jit_solution(16978504178929794533)
XLA Ops:
  7.2 0.0 all-gather.6.cloned.1.call-start
  7.2 0.7 all-gather.6.cloned.1.call-update
  7.9 0.0 all-gather.4.cloned.1.call-start
  7.9 0.7 convert_element_type.173
  8.6 37.6 %all-gather.6.cloned.1.call-done = bf16[1,256,5120]{2,1,0:T(8,128)(2,1)} async-done(((bf16[1,32,5120]{2,1,0:T(8,128)(2,1)}), bf16[1,256,5120]{2,1,0:T(8,128)(2,1)}) %all-gather.6.cloned.1.call-update) | async-done | bytes 2621456 | tf_op jit(solution)/shard_map/all_gather | solution.py:48
  46.3 2.3 fusion.9
  48.6 7.1 %fusion.32 = bf16[256,768]{1,0:T(8,128)(2,1)} fusion(bf16[5120,768]{1,0:T(8,128)(2,1)} %param.15, bf16[1,256,5120]{2,1,0:T(8,128)(2,1)} %all-gather.6.cloned.1.call-done, f32[5120]{0:T(1024)} %param.14, f32[256]{0:T(256)S(1)} %add_rsqrt_fusion.1, f32[768]{0:T(1024)S(1)} %convert_element_type.173), kind=kOutput, calls=%fused_computation.40 | convolution fusion | flops 2018902016 | bytes 10903552 | tf_op jit(solution)/shard_map/dot_general | solution.py:55
  55.7 0.0 all-gather.4.cloned.1.call-update
  56.5 0.5 copy.69
  57.0 1.3 copy.73
  58.4 0.5 copy.66
  58.9 1.3 copy.68
  60.3 0.5 multiply_cosine_fusion
  60.8 0.1 pad_maximum_fusion
  61.0 0.6 constant_dynamic-slice_fusion.1
  61.6 0.6 constant_dynamic-slice_fusion.2
  62.2 0.1 iota_compare_fusion
  62.3 0.1 pad_add_fusion
  62.4 30.8 %all-gather.4.cloned.1.call-done = bf16[256,6144]{1,0:T(8,128)(2,1)} async-done(((bf16[256,768]{1,0:T(8,128)(2,1)}), bf16[256,6144]{1,0:T(8,128)(2,1)}) %all-gather.4.cloned.1.call-update) | async-done | bytes 3145744 | tf_op jit(solution)/shard_map/all_gather | solution.py:58
  93.2 2.3 slice_bitcast_fusion
  95.5 0.2 copy.93
  95.7 0.7 constant_dynamic-slice_fusion
  96.3 0.3 fusion.56
  96.7 2.5 slice_convert_fusion
  99.1 5.6 %copy.75 = f32[256,4096]{0,1:T(8,128)} copy(f32[256,4096]{1,0:T(8,128)} %slice_convert_fusion) | data formatting | bytes 8388608 | tf_op jit(solution)/shard_map/convert_element_type | solution.py:25
  104.7 6.0 %reshape.139 = f32[256,8,4,128]{3,2,1,0:T(4,128)} reshape(f32[256,4096]{1,0:T(8,128)} %slice_convert_fusion) | data formatting | bytes 8388608 | tf_op jit(solution)/shard_map/convert_element_type | solution.py:25
  110.8 0.2 copy.90
  111.0 1.2 copy_negate_fusion
  112.2 1.2 copy-done
  113.3 1.7 slice_negate_fusion
  115.1 3.8 copy.76
  118.9 2.8 copy.77
  121.7 1.1 fusion.46
  122.8 13.2 %fusion = (f32[8,4,256]{2,1,0:T(4,128)S(1)}, f32[8,544,256,4]{2,1,3,0:T(8,128)}) fusion(pred[256,544]{0,1:T(8,128)(4,1)S(1)} %pad_add_fusion, f32[256,8,4,64]{3,0,2,1:T(8,128)} %copy.77, f32[256,8,4,64]{3,0,2,1:T(8,128)} %copy.76, f32[256,8,4,128]{3,2,1,0:T(4,128)} %reshape.139, f32[256,128]{1,0:T(8,128)S(1)} %get-tuple-element.18, ...), kind=kOutput, calls=%fused_computation.2 | convolution fusion | flops 1161682944 | bytes 27762688 | tf_op jit(solution)/shard_map/tkjd,skd->kjts/dot_general | solution.py:92
  136.1 10.5 %fusion.1 = bf16[8,4,256]{2,1,0:T(4,128)(2,1)S(1)} fusion(f32[8,544,256,4]{2,1,3,0:T(8,128)} %get-tuple-element.16, f32[8,4,256]{2,1,0:T(4,128)S(1)} %get-tuple-element.15, pred[256,544]{0,1:T(8,128)(4,1)S(1)} %pad_add_fusion), kind=kLoop, calls=%fused_computation.3 | loop fusion | flops 22274048 | bytes 18014208 | tf_op jit(solution)/shard_map/reduce_sum | solution.py:100
  146.6 0.5 broadcast.91
  147.1 0.7 reduce.6
  147.8 0.6 reshape.155
  148.5 3.3 all-to-all-start.2
  151.8 0.1 copy.92
  152.0 0.7 reduce.7
  152.7 0.6 reshape.153
  153.3 4.1 %all-to-all-done.2 = bf16[8,2,512]{2,1,0:T(2,128)(2,1)S(1)} async-done(((bf16[8,2,512]{2,1,0:T(2,128)(2,1)}), bf16[8,2,512]{2,1,0:T(2,128)(2,1)S(1)}, u32[]{:S(2)}, u32[]{:S(2)}) %all-to-all-start.2) | async-done | bytes 16416 | tf_op jit(solution)/shard_map/all_to_all | solution.py:115
  157.4 3.3 all-to-all-start.1
  160.7 9.4 %fusion.26 = bf16[8,128,4,256]{3,1,2,0:T(8,128)(2,1)} fusion(f32[8,544,256,4]{2,1,3,0:T(8,128)} %get-tuple-element.16, f32[8,4,256]{2,1,0:T(4,128)S(1)} %get-tuple-element.15, pred[256,544]{0,1:T(8,128)(4,1)S(1)} %pad_add_fusion, bf16[32,8,128]{2,0,1:T(8,128)(2,1)S(1)} %copy.87, bf16[512,8,128]{2,0,1:T(8,128)(2,1)S(1)} %copy-done.7), kind=kOutput, calls=%fused_computation.38 | convolution fusion | flops 1166409728 | bytes 21209088 | tf_op jit(solution)/shard_map/kjts,skd->tkjd/dot_general | solution.py:102
  170.2 5.0 %all-to-all-start = ((bf16[1,256,32,128]{1,3,0,2:T(8,128)(2,1)}), bf16[1,256,32,128]{1,3,0,2:T(8,128)(2,1)S(1)}, u32[]{:S(2)}, u32[]{:S(2)}) async-start(bf16[1,256,32,128]{1,3,0,2:T(8,128)(2,1)} %bitcast.122), calls=%async_computation | async-start | bytes 4194304 | tf_op jit(solution)/shard_map/all_to_all | solution.py:109
  175.2 0.0 all-reduce.2.cloned.1.call-start
  175.2 0.1 convert_reduce_fusion
  175.4 0.1 bitcast_reduce_fusion.1
  175.6 48.7 %all-to-all-done = bf16[1,256,32,128]{1,3,0,2:T(8,128)(2,1)S(1)} async-done(((bf16[1,256,32,128]{1,3,0,2:T(8,128)(2,1)}), bf16[1,256,32,128]{1,3,0,2:T(8,128)(2,1)S(1)}, u32[]{:S(2)}, u32[]{:S(2)}) %all-to-all-start) | async-done | bytes 2097184 | tf_op jit(solution)/shard_map/all_to_all | solution.py:109
  224.2 0.4 fusion.15
  224.7 5.7 %convolution_convert_fusion.1 = bf16[256,5120]{1,0:T(8,128)(2,1)} fusion(bf16[256,512]{0,1:T(8,128)(2,1)S(1)} %bitcast.123, bf16[512,5120]{1,0:T(8,128)(2,1)} %param.19), kind=kOutput, calls=%fused_computation.13 | convolution fusion | flops 1343488000 | bytes 8126464 | tf_op jit(solution)/shard_map/dot_general | solution.py:128
  230.4 0.0 all-reduce.2.cloned.1.call-update
  230.5 0.0 reduce-scatter.2.cloned.1.call-start
  230.5 68.1 %all-reduce.2.cloned.1.call-done = bf16[256,5120]{1,0:T(8,128)(2,1)} async-done(((bf16[256,5120]{1,0:T(8,128)(2,1)}), bf16[256,5120]{1,0:T(8,128)(2,1)}) %all-reduce.2.cloned.1.call-update) | async-done | bytes 2621456 | tf_op jit(solution)/shard_map/psum | solution.py:129
  298.7 2.9 fusion.6
  301.7 1.5 copy-done.2
  303.1 8.9 %fusion.40 = f32[256,1728]{0,1:T(8,128)S(1)} fusion(bf16[5120,1728]{0,1:T(8,128)(2,1)} %param.21, bf16[256,5120]{1,0:T(8,128)(2,1)S(1)} %get-tuple-element.4, f32[5120]{0:T(1024)S(1)} %copy-done.10, f32[256]{0:T(256)S(1)} %add_rsqrt_fusion), kind=kOutput, calls=%fused_computation.51 | convolution fusion | flops 4535091200 | bytes 22107136 | tf_op jit(solution)/shard_map/dot_general | solution.py:133
  312.0 28.5 %convolution_convert_fusion = bf16[256,5120]{1,0:T(8,128)(2,1)} fusion(bf16[1728,5120]{1,0:T(8,128)(2,1)} %param.23, bf16[5120,1728]{0,1:T(8,128)(2,1)} %param.22, f32[256,1728]{0,1:T(8,128)S(1)} %fusion.40, bf16[256,5120]{1,0:T(8,128)(2,1)} %copy-done.2, f32[5120]{0:T(1024)S(1)} %copy-done.10, f32[256]{0:T(256)S(1)} %add_rsqrt_fusion), kind=kOutput, calls=%fused_computation.12 | convolution fusion | flops 9068904448 | bytes 42423296 | tf_op jit(solution)/shard_map/dot_general | solution.py:137
  340.5 0.0 reduce-scatter.2.cloned.1.call-update
  340.6 0.7 reshape.137
  341.2 0.7 reshape.136
  341.9 35.2 %reduce-scatter.2.cloned.1.call-done = bf16[32,5120]{1,0:T(8,128)(2,1)} async-done(((bf16[256,5120]{1,0:T(8,128)(2,1)}), bf16[32,5120]{1,0:T(8,128)(2,1)}) %reduce-scatter.2.cloned.1.call-update) | async-done | bytes 327696 | tf_op jit(solution)/shard_map/reduce_scatter | solution.py:136
  377.1 1.9 fusion.42
  (42 shorter events, 0.4 us)
Async XLA Ops:
  7.2 39.1 %all-gather.6.cloned.1.call-start = ((), (), s32[]{:S(2)}) async-start(), calls=%async_computation.7 | async-start | bytes 2949120 | tf_op jit(solution)/shard_map/all_gather | solution.py:48
  7.9 85.3 %all-gather.4.cloned.1.call-start = ((), (), s32[]{:S(2)}) async-start(), calls=%async_computation.4 | async-start | bytes 3538944 | tf_op jit(solution)/shard_map/all_gather | solution.py:58
  48.6 7.9 %copy-start.5 = (bf16[1,512,1024]{2,1,0:T(8,128)(2,1)S(1)}, bf16[1,512,1024]{2,1,0:T(8,128)(2,1)}, u32[]{:S(2)}) copy-start(bf16[1,512,1024]{2,1,0:T(8,128)(2,1)} %param.17) | copy-start | bytes 3145732
  55.7 2.6 copy-start.6
  93.2 3.5 copy-start.3
  110.8 2.6 copy-start
  122.8 13.2 %copy-start.8 = (bf16[32,8,128]{2,0,1:T(8,128)(2,1)}, bf16[32,8,128]{2,0,1:T(8,128)(2,1)S(1)}, u32[]{:S(2)}) copy-start(bf16[32,8,128]{2,0,1:T(8,128)(2,1)S(1)} %fusion.46) | copy-start | bytes 196612
  136.1 15.7 %copy-start.4 = (bf16[32,8,8,128]{3,1,2,0:T(8,128)(2,1)S(1)}, bf16[32,8,8,128]{3,1,2,0:T(8,128)(2,1)}, u32[]{:S(2)}) copy-start(bf16[32,8,8,128]{3,1,2,0:T(8,128)(2,1)} %get-tuple-element.7) | copy-start | bytes 1572868
  136.1 24.6 %copy-start.7 = (bf16[512,8,128]{2,0,1:T(8,128)(2,1)S(1)}, bf16[512,8,128]{2,0,1:T(8,128)(2,1)}, u32[]{:S(2)}) copy-start(bf16[512,8,128]{2,0,1:T(8,128)(2,1)} %copy.68) | copy-start | bytes 3145732
  148.5 8.9 %all-to-all-start.2 = ((bf16[8,2,512]{2,1,0:T(2,128)(2,1)}), bf16[8,2,512]{2,1,0:T(2,128)(2,1)S(1)}, u32[]{:S(2)}, u32[]{:S(2)}) async-start(bf16[8,2,512]{2,1,0:T(2,128)(2,1)} %reshape.155), calls=%async_computation.2 | async-start | bytes 32768 | tf_op jit(solution)/shard_map/all_to_all | solution.py:115
  157.4 12.8 %all-to-all-start.1 = ((bf16[8,2,512]{2,1,0:T(2,128)(2,1)}), bf16[8,2,512]{2,1,0:T(2,128)(2,1)S(1)}, u32[]{:S(2)}, u32[]{:S(2)}) async-start(bf16[8,2,512]{2,1,0:T(2,128)(2,1)} %reshape.153), calls=%async_computation.1 | async-start | bytes 32768 | tf_op jit(solution)/shard_map/all_to_all | solution.py:112
  170.2 54.1 %all-to-all-start = ((bf16[1,256,32,128]{1,3,0,2:T(8,128)(2,1)}), bf16[1,256,32,128]{1,3,0,2:T(8,128)(2,1)S(1)}, u32[]{:S(2)}, u32[]{:S(2)}) async-start(bf16[1,256,32,128]{1,3,0,2:T(8,128)(2,1)} %bitcast.122), calls=%async_computation | async-start | bytes 4194304 | tf_op jit(solution)/shard_map/all_to_all | solution.py:109
  175.2 123.5 %all-reduce.2.cloned.1.call-start = ((), (), s32[]{:S(2)}) async-start(), calls=%async_computation.5 | async-start | bytes 5242880 | tf_op jit(solution)/shard_map/psum | solution.py:129
  224.7 74.0 %copy-start.1 = (bf16[1,256,5120]{2,1,0:T(8,128)(2,1)S(1)}, bf16[1,256,5120]{2,1,0:T(8,128)(2,1)}, u32[]{:S(2)}) copy-start(bf16[1,256,5120]{2,1,0:T(8,128)(2,1)} %all-gather.6.cloned.1.call-done) | copy-start | bytes 7864324
  230.5 72.7 %copy-start.10 = (f32[5120]{0:T(1024)S(1)}, f32[5120]{0:T(1024)}, u32[]{:S(2)}) copy-start(f32[5120]{0:T(1024)} %param.20) | copy-start | bytes 61444
  230.5 146.6 %reduce-scatter.2.cloned.1.call-start = ((), (), s32[]{:S(2)}) async-start(), calls=%async_computation.6 | async-start | bytes 2949120 | tf_op jit(solution)/shard_map/reduce_scatter | solution.py:136
  301.6 1.5 copy-start.2
  312.0 28.5 %copy-start.9 = (bf16[32,8,128]{2,0,1:T(8,128)(2,1)S(1)}, bf16[32,8,128]{2,0,1:T(8,128)(2,1)}, u32[]{:S(2)}) copy-start(bf16[32,8,128]{2,0,1:T(8,128)(2,1)} %copy-done.8) | copy-start | bytes 196612
Sparse Core Ops, SparseCore 0:
  9.6 36.5 all-gather.5
  55.9 37.2 all-gather.3
  230.6 68.0 all-reduce.1
  340.6 36.4 reduce-scatter.1
where the time goes:
time: 386 us; the launch traced here: 385 us
  waiting for transfers between devices  225 us (58%)
  matrix products  72.8 us (19%)
  local copies, waits for them, and re-layouts  30.7 us (8%)
  other arithmetic  30.1 us (8%)
  between operations  14.8 us (4%)
  starting transfers between devices  11.8 us (3%)
    psum x1, waiting for transfers between devices, on_device(): lax.psum(projected.astype(jnp.bfloat16), 'head').astype(jnp.float32)  68.1 us
    all_to_all x1, waiting for transfers between devices, on_device(): lax.all_to_all(weighted[None].astype(jnp.bfloat16), 'head', split_axis=2,...  48.7 us
    all_gather x1, waiting for transfers between devices, on_device(): all_rows = lax.all_gather(own_rows, 'head', axis=0, tiled=True)  37.6 us
    reduce_scatter x1, waiting for transfers between devices, on_device(): lax.psum_scatter(jnp.dot(active, w_down, preferred_element_type=jnp.float...  35.2 us
    all_gather x1, waiting for transfers between devices, on_device(): query_key_value = lax.all_gather(qkv_part, 'head', axis=1, tiled=True)  30.8 us
    dot_general x1, matrix products, on_device(): jnp.dot(active, w_down, preferred_element_type=jnp.float32)  28.5 us
    dot_general x1, matrix products, on_device(): jnp.einsum('tkjd,skd->kjts', grouped_queries, joined_keys, preferred_elem...  13.2 us
    convert_element_type x2, local copies, waits for them, and re-layouts, rope_apply(): data = values.astype(jnp.float32)  11.6 us
  transfers between devices with their start and end apart: 7, of which 6 were waited for; matrix products, arithmetic and copies ran while one was open for 5% of the time, Pallas kernels for 0%

commit v1 on v0

--- a/solution.py
+++ b/solution.py
@@ -45,7 +45,12 @@
     index_here = lax.axis_index("head")
     own_rows = hidden[0]
     fresh_count = own_rows.shape[0]
-    all_rows = lax.all_gather(own_rows, "head", axis=0, tiled=True)
+    ring = [own_rows]
+    for hop in range(7):
+        ring.append(lax.ppermute(ring[-1], "head", [(dev, (dev + 1) % 8) for dev in range(8)]))
+    all_rows = jnp.roll(
+        jnp.concatenate(ring[::-1], axis=0), (lax.axis_index("head") + 1) * ring[0].shape[0], axis=0
+    )
     token_total = all_rows.shape[0]
     head_group = QUERY_HEADS // KEY_VALUE_HEADS
     heads_here = QUERY_HEADS // group_size

time: 386 us -> 403 us (1.044)
  waiting for transfers between devices: 225 us -> 245 us
  matrix products: 72.8 us -> 67.8 us
    ppermute x0 -> x7, waiting for transfers between devices: none -> 58.1 us  [on_device(): lax.ppermute(ring[-1], 'head', [(dev, (dev + 1) % 8) for dev in range(8)])]
    all_gather x1 -> x0, waiting for transfers between devices: 37.6 us -> none  [on_device(): all_rows = lax.all_gather(own_rows, 'head', axis=0, tiled=True)]
    dot_general x1, matrix products: 7.12 us -> 3.01 us  [on_device(): jnp.dot(normed, query_key_value_weight, preferred_element_type=jnp.float32)]
    unnamed x33 -> x52, local copies, waits for them, and re-layouts: 6.07 us -> 9.13 us
  transfers between devices with their start and end apart: 7 -> 13, of which waited for: 6 -> 12; matrix products, arithmetic and copies ran while one was open for 5% -> 5% of each run, Pallas kernels for 0% -> 0%
where the time goes in v1:
time: 403 us; the launch traced here: 402 us
  waiting for transfers between devices  245 us (61%)
  matrix products  67.8 us (17%)
  local copies, waits for them, and re-layouts  33.8 us (8%)
  other arithmetic  29 us (7%)
  between operations  14.9 us (4%)
  starting transfers between devices  12.3 us (3%)
    psum x1, waiting for transfers between devices, on_device(): lax.psum(projected.astype(jnp.bfloat16), 'head').astype(jnp.float32)  68.1 us
    ppermute x7, waiting for transfers between devices, on_device(): lax.ppermute(ring[-1], 'head', [(dev, (dev + 1) % 8) for dev in range(8)])  58.1 us
    all_to_all x1, waiting for transfers between devices, on_device(): lax.all_to_all(weighted[None].astype(jnp.bfloat16), 'head', split_axis=2,...  48.7 us
    reduce_scatter x1, waiting for transfers between devices, on_device(): lax.psum_scatter(jnp.dot(active, w_down, preferred_element_type=jnp.float...  35.1 us
    all_gather x1, waiting for transfers between devices, on_device(): query_key_value = lax.all_gather(qkv_part, 'head', axis=1, tiled=True)  30.5 us
    dot_general x1, matrix products, on_device(): jnp.dot(active, w_down, preferred_element_type=jnp.float32)  26.5 us
    dot_general x1, matrix products, on_device(): jnp.einsum('tkjd,skd->kjts', grouped_queries, joined_keys, preferred_elem...  13.2 us
    convert_element_type x2, local copies, waits for them, and re-layouts, rope_apply(): data = values.astype(jnp.float32)  11.6 us
  transfers between devices with their start and end apart: 13, of which 12 were waited for; matrix products, arithmetic and copies ran while one was open for 5% of the time, Pallas kernels for 0%

profile of v1, /device:TPU:0, one launch (start us, length us, event | category | flops | bytes accessed | tf_op | source)
XLA Modules:
  0.0 402.5 jit_solution(16297297512734361608)
XLA Ops:
  7.2 0.5 collective-permute-start
  7.7 9.0 %collective-permute-done = bf16[32,5120]{1,0:T(8,128)(2,1)S(1)} collective-permute-done((bf16[32,5120]{1,0:T(8,128)(2,1)}, bf16[32,5120]{1,0:T(8,128)(2,1)S(1)}, u32[]{:S(2)}, u32[]{:S(2)}) %collective-permute-start) | collective-permute-done | bytes 327712 | tf_op jit(solution)/shard_map/ppermute | solution.py:50
  16.7 8.3 %collective-permute-done.1 = bf16[32,5120]{1,0:T(8,128)(2,1)S(1)} collective-permute-done((bf16[32,5120]{1,0:T(8,128)(2,1)S(1)}, bf16[32,5120]{1,0:T(8,128)(2,1)S(1)}, u32[]{:S(2)}, u32[]{:S(2)}) %collective-permute-start.1) | collective-permute-done | bytes 327712 | tf_op jit(solution)/shard_map/ppermute | solution.py:50
  25.0 8.3 %collective-permute-done.2 = bf16[32,5120]{1,0:T(8,128)(2,1)S(1)} collective-permute-done((bf16[32,5120]{1,0:T(8,128)(2,1)S(1)}, bf16[32,5120]{1,0:T(8,128)(2,1)S(1)}, u32[]{:S(2)}, u32[]{:S(2)}) %collective-permute-start.2) | collective-permute-done | bytes 327712 | tf_op jit(solution)/shard_map/ppermute | solution.py:50
  33.3 8.3 %collective-permute-done.3 = bf16[32,5120]{1,0:T(8,128)(2,1)S(1)} collective-permute-done((bf16[32,5120]{1,0:T(8,128)(2,1)S(1)}, bf16[32,5120]{1,0:T(8,128)(2,1)S(1)}, u32[]{:S(2)}, u32[]{:S(2)}) %collective-permute-start.3) | collective-permute-done | bytes 327712 | tf_op jit(solution)/shard_map/ppermute | solution.py:50
  41.6 8.3 %collective-permute-done.4 = bf16[32,5120]{1,0:T(8,128)(2,1)S(1)} collective-permute-done((bf16[32,5120]{1,0:T(8,128)(2,1)S(1)}, bf16[32,5120]{1,0:T(8,128)(2,1)S(1)}, u32[]{:S(2)}, u32[]{:S(2)}) %collective-permute-start.4) | collective-permute-done | bytes 327712 | tf_op jit(solution)/shard_map/ppermute | solution.py:50
  49.9 8.3 %collective-permute-done.5 = bf16[32,5120]{1,0:T(8,128)(2,1)S(1)} collective-permute-done((bf16[32,5120]{1,0:T(8,128)(2,1)S(1)}, bf16[32,5120]{1,0:T(8,128)(2,1)S(1)}, u32[]{:S(2)}, u32[]{:S(2)}) %collective-permute-start.5) | collective-permute-done | bytes 327712 | tf_op jit(solution)/shard_map/ppermute | solution.py:50
  58.2 0.7 convert_element_type.173
  58.9 7.6 %collective-permute-done.6 = bf16[32,5120]{1,0:T(8,128)(2,1)S(1)} collective-permute-done((bf16[32,5120]{1,0:T(8,128)(2,1)S(1)}, bf16[32,5120]{1,0:T(8,128)(2,1)S(1)}, u32[]{:S(2)}, u32[]{:S(2)}) %collective-permute-start.6) | collective-permute-done | bytes 327712 | tf_op jit(solution)/shard_map/ppermute | solution.py:50
  66.8 1.1 constant_dynamic-update-slice_fusion.8
  68.2 0.6 fusion.9
  68.8 2.0 copy-done.1
  70.8 1.0 copy-done.10
  71.9 3.0 fusion.32
  75.7 0.5 copy.69
  76.2 1.3 copy.73
  77.5 0.5 copy.66
  78.1 1.3 copy.68
  79.4 0.5 multiply_cosine_fusion
  80.0 0.1 pad_maximum_fusion
  80.1 0.6 constant_dynamic-slice_fusion
  80.7 0.6 constant_dynamic-slice_fusion.2
  81.4 0.1 pad_add_fusion
  81.6 30.5 %all-gather.2.cloned.1.call-done = bf16[256,6144]{1,0:T(8,128)(2,1)} async-done(((bf16[256,768]{1,0:T(8,128)(2,1)}), bf16[256,6144]{1,0:T(8,128)(2,1)}) %all-gather.2.cloned.1.call-update) | async-done | bytes 3145744 | tf_op jit(solution)/shard_map/all_gather | solution.py:63
  112.1 2.3 slice_bitcast_fusion
  114.3 0.2 copy.93
  114.5 0.3 fusion.57
  114.9 0.7 constant_dynamic-slice_fusion.1
  115.6 2.5 slice_convert_fusion
  118.0 5.6 %copy.75 = f32[256,4096]{0,1:T(8,128)} copy(f32[256,4096]{1,0:T(8,128)} %slice_convert_fusion) | data formatting | bytes 8388608 | tf_op jit(solution)/shard_map/convert_element_type | solution.py:25
  123.6 6.0 %reshape.139 = f32[256,8,4,128]{3,2,1,0:T(4,128)} reshape(f32[256,4096]{1,0:T(8,128)} %slice_convert_fusion) | data formatting | bytes 8388608 | tf_op jit(solution)/shard_map/convert_element_type | solution.py:25
  129.6 0.2 copy.90
  129.8 1.2 copy_negate_fusion
  131.0 1.1 copy-done
  132.2 1.8 slice_negate_fusion
  133.9 3.9 copy.76
  137.8 2.7 copy.77
  140.6 1.1 fusion.46
  141.7 13.2 %fusion = (f32[8,4,256]{2,1,0:T(4,128)S(1)}, f32[8,544,256,4]{2,1,3,0:T(8,128)}) fusion(pred[256,544]{0,1:T(8,128)(4,1)S(1)} %pad_add_fusion, f32[256,8,4,64]{3,0,2,1:T(8,128)} %copy.77, f32[256,8,4,64]{3,0,2,1:T(8,128)} %copy.76, f32[256,8,4,128]{3,2,1,0:T(4,128)} %reshape.139, f32[256,128]{1,0:T(8,128)S(1)} %get-tuple-element.18, ...), kind=kOutput, calls=%fused_computation.2 | convolution fusion | flops 1161682944 | bytes 27762688 | tf_op jit(solution)/shard_map/tkjd,skd->kjts/dot_general | solution.py:97
  154.9 10.5 %fusion.1 = bf16[8,4,256]{2,1,0:T(4,128)(2,1)S(1)} fusion(f32[8,544,256,4]{2,1,3,0:T(8,128)} %get-tuple-element.16, f32[8,4,256]{2,1,0:T(4,128)S(1)} %get-tuple-element.15, pred[256,544]{0,1:T(8,128)(4,1)S(1)} %pad_add_fusion), kind=kLoop, calls=%fused_computation.3 | loop fusion | flops 22274048 | bytes 18014208 | tf_op jit(solution)/shard_map/reduce_sum | solution.py:105
  165.4 0.5 broadcast.92
  165.9 0.7 reduce.6
  166.7 0.6 reshape.153
  167.3 3.3 all-to-all-start.2
  170.6 0.1 copy.92
  170.8 0.7 reduce.7
  171.5 0.6 reshape.151
  172.2 4.1 %all-to-all-done.2 = bf16[8,2,512]{2,1,0:T(2,128)(2,1)S(1)} async-done(((bf16[8,2,512]{2,1,0:T(2,128)(2,1)}), bf16[8,2,512]{2,1,0:T(2,128)(2,1)S(1)}, u32[]{:S(2)}, u32[]{:S(2)}) %all-to-all-start.2) | async-done | bytes 16416 | tf_op jit(solution)/shard_map/all_to_all | solution.py:120
  176.2 3.3 all-to-all-start.1
  179.6 9.4 %fusion.26 = bf16[8,128,4,256]{3,1,2,0:T(8,128)(2,1)} fusion(f32[8,544,256,4]{2,1,3,0:T(8,128)} %get-tuple-element.16, f32[8,4,256]{2,1,0:T(4,128)S(1)} %get-tuple-element.15, pred[256,544]{0,1:T(8,128)(4,1)S(1)} %pad_add_fusion, bf16[32,8,128]{2,0,1:T(8,128)(2,1)S(1)} %copy.87, bf16[512,8,128]{2,0,1:T(8,128)(2,1)S(1)} %copy-done.7), kind=kOutput, calls=%fused_computation.38 | convolution fusion | flops 1166409728 | bytes 21209088 | tf_op jit(solution)/shard_map/kjts,skd->tkjd/dot_general | solution.py:107
  189.0 5.0 %all-to-all-start = ((bf16[1,256,32,128]{1,3,0,2:T(8,128)(2,1)}), bf16[1,256,32,128]{1,3,0,2:T(8,128)(2,1)S(1)}, u32[]{:S(2)}, u32[]{:S(2)}) async-start(bf16[1,256,32,128]{1,3,0,2:T(8,128)(2,1)} %bitcast.112), calls=%async_computation | async-start | bytes 4194304 | tf_op jit(solution)/shard_map/all_to_all | solution.py:114
  194.1 0.1 convert_reduce_fusion
  194.2 0.1 bitcast_reduce_fusion.1
  194.4 48.7 %all-to-all-done = bf16[1,256,32,128]{1,3,0,2:T(8,128)(2,1)S(1)} async-done(((bf16[1,256,32,128]{1,3,0,2:T(8,128)(2,1)}), bf16[1,256,32,128]{1,3,0,2:T(8,128)(2,1)S(1)}, u32[]{:S(2)}, u32[]{:S(2)}) %all-to-all-start) | async-done | bytes 2097184 | tf_op jit(solution)/shard_map/all_to_all | solution.py:114
  243.1 0.4 fusion.15
  243.5 5.5 %convolution_convert_fusion.1 = bf16[256,5120]{1,0:T(8,128)(2,1)} fusion(bf16[256,512]{0,1:T(8,128)(2,1)S(1)} %bitcast.113, bf16[512,5120]{1,0:T(8,128)(2,1)} %param.19), kind=kOutput, calls=%fused_computation.13 | convolution fusion | flops 1343488000 | bytes 8126464 | tf_op jit(solution)/shard_map/dot_general | solution.py:133
  249.2 68.1 %all-reduce.2.cloned.1.call-done = bf16[256,5120]{1,0:T(8,128)(2,1)} async-done(((bf16[256,5120]{1,0:T(8,128)(2,1)}), bf16[256,5120]{1,0:T(8,128)(2,1)}) %all-reduce.2.cloned.1.call-update) | async-done | bytes 2621456 | tf_op jit(solution)/shard_map/psum | solution.py:134
  317.3 3.7 fusion.6
  321.1 10.2 %fusion.40 = f32[256,1728]{0,1:T(8,128)} fusion(bf16[5120,1728]{0,1:T(8,128)(2,1)} %param.21, bf16[256,5120]{1,0:T(8,128)(2,1)S(1)} %get-tuple-element.4, f32[5120]{0:T(1024)S(1)} %copy-done.12, f32[256]{0:T(256)S(1)} %add_rsqrt_fusion), kind=kOutput, calls=%fused_computation.51 | convolution fusion | flops 4535091200 | bytes 22107136 | tf_op jit(solution)/shard_map/dot_general | solution.py:138
  331.2 26.5 %convolution_convert_fusion = bf16[256,5120]{1,0:T(8,128)(2,1)} fusion(bf16[1728,5120]{1,0:T(8,128)(2,1)} %param.23, bf16[5120,1728]{0,1:T(8,128)(2,1)} %param.22, f32[256,1728]{0,1:T(8,128)} %fusion.40, bf16[256,5120]{1,0:T(8,128)(2,1)S(1)} %get-tuple-element.4, f32[5120]{0:T(1024)S(1)} %copy-done.12, f32[256]{0:T(256)S(1)} %add_rsqrt_fusion), kind=kOutput, calls=%fused_computation.12 | convolution fusion | flops 9068904448 | bytes 42423296 | tf_op jit(solution)/shard_map/dot_general | solution.py:142
  357.8 0.7 reshape.137
  358.4 0.7 reshape.136
  359.1 35.1 %reduce-scatter.2.cloned.1.call-done = bf16[32,5120]{1,0:T(8,128)(2,1)} async-done(((bf16[256,5120]{1,0:T(8,128)(2,1)}), bf16[32,5120]{1,0:T(8,128)(2,1)}) %reduce-scatter.2.cloned.1.call-update) | async-done | bytes 327696 | tf_op jit(solution)/shard_map/reduce_scatter | solution.py:141
  394.2 1.8 fusion.42
  (73 shorter events, 1.0 us)
Async XLA Ops:
  7.2 61.0 %copy-start.4 = (bf16[1,32,5120]{2,1,0:T(8,128)(2,1)S(1)}, bf16[1,32,5120]{2,1,0:T(8,128)(2,1)}, u32[]{:S(2)}) copy-start(bf16[1,32,5120]{2,1,0:T(8,128)(2,1)} %param.12) | copy-start | bytes 983044
  7.2 104.9 %all-gather.2.cloned.1.call-start = ((), (), s32[]{:S(2)}) async-start(), calls=%async_computation.4 | async-start | bytes 3538944 | tf_op jit(solution)/shard_map/all_gather | solution.py:63
  7.2 9.5 %collective-permute-start = (bf16[32,5120]{1,0:T(8,128)(2,1)}, bf16[32,5120]{1,0:T(8,128)(2,1)S(1)}, u32[]{:S(2)}, u32[]{:S(2)}) collective-permute-start(bf16[32,5120]{1,0:T(8,128)(2,1)} %bitcast.114), channel_id=1, source_target_pairs={{0,1},{1,2},{2,3},{3,4},{4,5},{5,6},{6,7},{7,0},{8,9},{9,10},{10,1... | collective-permute-start | bytes 983048 | tf_op jit(solution)/shard_map/ppermute | solution.py:50
  16.7 8.3 %collective-permute-start.1 = (bf16[32,5120]{1,0:T(8,128)(2,1)S(1)}, bf16[32,5120]{1,0:T(8,128)(2,1)S(1)}, u32[]{:S(2)}, u32[]{:S(2)}) collective-permute-start(bf16[32,5120]{1,0:T(8,128)(2,1)S(1)} %collective-permute-done), channel_id=1, source_target_pairs={{0,1},{1,2},{2,3},{3,4},{4,5},{5,6},{6,7},{7,0},{8,9},{9,10},{10,1... | collective-permute-start | bytes 983048 | tf_op jit(solution)/shard_map/ppermute | solution.py:50
  25.0 8.3 %collective-permute-start.2 = (bf16[32,5120]{1,0:T(8,128)(2,1)S(1)}, bf16[32,5120]{1,0:T(8,128)(2,1)S(1)}, u32[]{:S(2)}, u32[]{:S(2)}) collective-permute-start(bf16[32,5120]{1,0:T(8,128)(2,1)S(1)} %collective-permute-done.1), channel_id=1, source_target_pairs={{0,1},{1,2},{2,3},{3,4},{4,5},{5,6},{6,7},{7,0},{8,9},{9,10},{10,1... | collective-permute-start | bytes 983048 | tf_op jit(solution)/shard_map/ppermute | solution.py:50
  33.3 8.3 %collective-permute-start.3 = (bf16[32,5120]{1,0:T(8,128)(2,1)S(1)}, bf16[32,5120]{1,0:T(8,128)(2,1)S(1)}, u32[]{:S(2)}, u32[]{:S(2)}) collective-permute-start(bf16[32,5120]{1,0:T(8,128)(2,1)S(1)} %collective-permute-done.2), channel_id=1, source_target_pairs={{0,1},{1,2},{2,3},{3,4},{4,5},{5,6},{6,7},{7,0},{8,9},{9,10},{10,1... | collective-permute-start | bytes 983048 | tf_op jit(solution)/shard_map/ppermute | solution.py:50
  41.6 8.3 %collective-permute-start.4 = (bf16[32,5120]{1,0:T(8,128)(2,1)S(1)}, bf16[32,5120]{1,0:T(8,128)(2,1)S(1)}, u32[]{:S(2)}, u32[]{:S(2)}) collective-permute-start(bf16[32,5120]{1,0:T(8,128)(2,1)S(1)} %collective-permute-done.3), channel_id=1, source_target_pairs={{0,1},{1,2},{2,3},{3,4},{4,5},{5,6},{6,7},{7,0},{8,9},{9,10},{10,1... | collective-permute-start | bytes 983048 | tf_op jit(solution)/shard_map/ppermute | solution.py:50
  49.9 8.3 %collective-permute-start.5 = (bf16[32,5120]{1,0:T(8,128)(2,1)S(1)}, bf16[32,5120]{1,0:T(8,128)(2,1)S(1)}, u32[]{:S(2)}, u32[]{:S(2)}) collective-permute-start(bf16[32,5120]{1,0:T(8,128)(2,1)S(1)} %collective-permute-done.4), channel_id=1, source_target_pairs={{0,1},{1,2},{2,3},{3,4},{4,5},{5,6},{6,7},{7,0},{8,9},{9,10},{10,1... | collective-permute-start | bytes 983048 | tf_op jit(solution)/shard_map/ppermute | solution.py:50
  58.2 8.3 %collective-permute-start.6 = (bf16[32,5120]{1,0:T(8,128)(2,1)S(1)}, bf16[32,5120]{1,0:T(8,128)(2,1)S(1)}, u32[]{:S(2)}, u32[]{:S(2)}) collective-permute-start(bf16[32,5120]{1,0:T(8,128)(2,1)S(1)} %collective-permute-done.5), channel_id=1, source_target_pairs={{0,1},{1,2},{2,3},{3,4},{4,5},{5,6},{6,7},{7,0},{8,9},{9,10},{10,1... | collective-permute-start | bytes 983048 | tf_op jit(solution)/shard_map/ppermute | solution.py:50
  66.6 5.2 %copy-start.10 = (bf16[5120,768]{1,0:T(8,128)(2,1)S(1)}, bf16[5120,768]{1,0:T(8,128)(2,1)}, u32[]{:S(2)}) copy-start(bf16[5120,768]{1,0:T(8,128)(2,1)} %param.15) | copy-start | bytes 23592964
  66.7 5.2 %copy-start.11 = (f32[5120]{0:T(1024)S(1)}, f32[5120]{0:T(1024)}, u32[]{:S(2)}) copy-start(f32[5120]{0:T(1024)} %param.14) | copy-start | bytes 61444
  68.2 2.7 copy-start.1
  71.9 3.8 copy-start.5
  74.9 2.7 copy-start.6
  112.1 3.5 copy-start.2
  129.6 2.6 copy-start
  141.6 13.2 %copy-start.8 = (bf16[32,8,128]{2,0,1:T(8,128)(2,1)}, bf16[32,8,128]{2,0,1:T(8,128)(2,1)S(1)}, u32[]{:S(2)}) copy-start(bf16[32,8,128]{2,0,1:T(8,128)(2,1)S(1)} %fusion.46) | copy-start | bytes 196612
  154.9 15.7 %copy-start.3 = (bf16[32,8,8,128]{3,1,2,0:T(8,128)(2,1)S(1)}, bf16[32,8,8,128]{3,1,2,0:T(8,128)(2,1)}, u32[]{:S(2)}) copy-start(bf16[32,8,8,128]{3,1,2,0:T(8,128)(2,1)} %get-tuple-element.7) | copy-start | bytes 1572868
  154.9 24.6 %copy-start.7 = (bf16[512,8,128]{2,0,1:T(8,128)(2,1)S(1)}, bf16[512,8,128]{2,0,1:T(8,128)(2,1)}, u32[]{:S(2)}) copy-start(bf16[512,8,128]{2,0,1:T(8,128)(2,1)} %copy.68) | copy-start | bytes 3145732
  167.3 8.9 %all-to-all-start.2 = ((bf16[8,2,512]{2,1,0:T(2,128)(2,1)}), bf16[8,2,512]{2,1,0:T(2,128)(2,1)S(1)}, u32[]{:S(2)}, u32[]{:S(2)}) async-start(bf16[8,2,512]{2,1,0:T(2,128)(2,1)} %reshape.153), calls=%async_computation.2 | async-start | bytes 32768 | tf_op jit(solution)/shard_map/all_to_all | solution.py:120
  176.2 12.8 %all-to-all-start.1 = ((bf16[8,2,512]{2,1,0:T(2,128)(2,1)}), bf16[8,2,512]{2,1,0:T(2,128)(2,1)S(1)}, u32[]{:S(2)}, u32[]{:S(2)}) async-start(bf16[8,2,512]{2,1,0:T(2,128)(2,1)} %reshape.151), calls=%async_computation.1 | async-start | bytes 32768 | tf_op jit(solution)/shard_map/all_to_all | solution.py:117
  189.0 54.1 %all-to-all-start = ((bf16[1,256,32,128]{1,3,0,2:T(8,128)(2,1)}), bf16[1,256,32,128]{1,3,0,2:T(8,128)(2,1)S(1)}, u32[]{:S(2)}, u32[]{:S(2)}) async-start(bf16[1,256,32,128]{1,3,0,2:T(8,128)(2,1)} %bitcast.112), calls=%async_computation | async-start | bytes 4194304 | tf_op jit(solution)/shard_map/all_to_all | solution.py:114
  194.0 123.3 %all-reduce.2.cloned.1.call-start = ((), (), s32[]{:S(2)}) async-start(), calls=%async_computation.5 | async-start | bytes 5242880 | tf_op jit(solution)/shard_map/psum | solution.py:134
  249.1 72.0 %copy-start.12 = (f32[5120]{0:T(1024)S(1)}, f32[5120]{0:T(1024)}, u32[]{:S(2)}) copy-start(f32[5120]{0:T(1024)} %param.20) | copy-start | bytes 61444
  249.1 145.1 %reduce-scatter.2.cloned.1.call-start = ((), (), s32[]{:S(2)}) async-start(), calls=%async_computation.6 | async-start | bytes 2949120 | tf_op jit(solution)/shard_map/reduce_scatter | solution.py:141
  331.2 26.5 %copy-start.9 = (bf16[32,8,128]{2,0,1:T(8,128)(2,1)S(1)}, bf16[32,8,128]{2,0,1:T(8,128)(2,1)}, u32[]{:S(2)}) copy-start(bf16[32,8,128]{2,0,1:T(8,128)(2,1)} %copy-done.8) | copy-start | bytes 196612
Sparse Core Ops, SparseCore 0:
  75.0 36.9 all-gather.1
  249.2 68.0 all-reduce.1
  357.8 36.2 reduce-scatter.1
